TPU v7x, 512 devices: a whole 4x8x8 slice. The times are simulated.
512 devices in a mesh: pts: 128 (over x, z, y_lo, core), lmk: 4 (over y_hi).
Axes of the slice: x: 4, y: 8 (y_hi: 4, y_lo: 2; y = y_hi * 2 + y_lo), z: 8, core: 2. Of those that a mesh axis runs over, the one named last changes fastest.
Arguments:
- points: bfloat16 [32768, 768], P('pts'), may hold values from -6 to 6
- landmarks: bfloat16 [384, 768], P('lmk'), may hold values from -6 to 6
- panels: bfloat16 [128, 384, 2048], P('pts', None, 'lmk'), may hold values from -0.3125 to 0.3125
- panel_index: int32 [1], replicated, may hold values from 0 to 127
- assignment: int32 [32768], P('pts'), may hold values from 0 to 4095, as said below
Outputs:
- centroid_sums: float32 [4096, 2048], P('pts', 'lmk')
- cluster_counts: int32 [4096], P('pts')
Inputs may be any that keep to these rules, and one draw needn't show every extreme that they name: `assignment`: owner of a cluster c is c // 32. In each aligned block of 256 points (the points of one device) at most 4 points have clusters of one owner; one owner, the same for every block, has exactly 4 points in every block.
All inputs are finite; a program needn't handle non-finite values.
Results may differ from a plain program's by a relative error of at most 0.0017.
Values may be sent and summed in bfloat16 or wider, within the bound.
A program may use at most 64 MiB of HBM per device.

v0:
```python
import math

import jax
import jax.numpy as jnp
from jax import lax
from jax.sharding import PartitionSpec as P

CLUSTERS = 4096


def spread(block, axis, holder):
    block = jnp.where(lax.axis_index(axis) == holder, block, jnp.zeros_like(block))
    return lax.psum(block, axis)


def unit_rows(values_in):
    widened = values_in.astype(jnp.float32)
    scale = lax.rsqrt(jnp.mean(widened * widened, axis=1, keepdims=True) + 1e-06)
    return (widened * scale).astype(jnp.bfloat16)


def kernel_rows(unit_points, unit_marks):
    scores = lax.dot_general(
        unit_points, unit_marks, (((1,), (1,)), ((), ())), preferred_element_type=jnp.float32
    )
    return jnp.exp(scores * (0.5 / math.sqrt(unit_points.shape[1]))).astype(jnp.bfloat16)


def body(points, landmarks, panels, panel_index, assignment):
    point_groups = lax.axis_size("pts")
    point_rows = points.shape[0]
    unit_points = unit_rows(points)
    kernel = kernel_rows(
        unit_points, unit_rows(lax.all_gather(landmarks, "lmk", axis=0, tiled=True))
    )
    factor_panel = spread(panels[0], "pts", panel_index[0])
    owned_clusters = CLUSTERS // point_groups
    capacity = 2 * point_rows // point_groups
    owners = assignment // owned_clusters
    local_id = assignment - owners * owned_clusters
    owner_hits = (owners[:, None] == jnp.arange(point_groups, dtype=jnp.int32)[None, :]).astype(
        jnp.int32
    )
    slot_rank = jnp.sum(jnp.cumsum(owner_hits, axis=0) * owner_hits, axis=1) - 1
    slot_ids = jnp.full((point_groups, capacity), -1, jnp.int32).at[owners, slot_rank].set(local_id)
    features = jnp.dot(kernel, factor_panel, preferred_element_type=jnp.float32).astype(
        jnp.bfloat16
    )
    slots = (
        jnp.zeros((point_groups, capacity, features.shape[1]), jnp.bfloat16)
        .at[owners, slot_rank]
        .set(features)
    )
    arrived, arrived_ids = (
        lax.all_to_all(slots, "pts", split_axis=0, concat_axis=0, tiled=True),
        lax.all_to_all(slot_ids, "pts", split_axis=0, concat_axis=0, tiled=True),
    )
    received = arrived.reshape(-1, arrived.shape[2])
    membership = (
        arrived_ids.reshape(-1)[None, :] == jnp.arange(owned_clusters, dtype=jnp.int32)[:, None]
    )
    totals = jnp.dot(membership.astype(jnp.bfloat16), received, preferred_element_type=jnp.float32)
    counts = jnp.sum(membership.astype(jnp.int32), axis=1)
    mean_count = point_rows * point_groups / CLUSTERS
    return (totals / mean_count, counts)


def solution(mesh):
    in_specs = (P("pts", None), P("lmk", None), P("pts", None, "lmk"), P(), P("pts"))
    out_specs = (P("pts", "lmk"), P("pts"))
    return jax.shard_map(body, mesh=mesh, in_specs=in_specs, out_specs=out_specs, check_vma=False)
```

profile of v0, /device:TPU:1, one launch (start us, length us, event | category | flops | bytes accessed | tf_op | source)
XLA Modules:
  0.0 1064.7 jit_solution(14033932260171003460)
XLA Ops:
  7.2 0.0 all-reduce.2.cloned.1.call-start
  7.9 0.8 select_bitcast_fusion
  8.7 0.0 all-reduce.2.cloned.1.call-update
  8.7 0.1 copy.13
  8.8 0.2 fusion.15
  9.1 0.2 fusion.16
  9.4 11.1 %scatter_fusion = s32[128,4]{0,1:T(4,128)S(1)} fusion(s32[128,4]{0,1:T(4,128)S(1)} %broadcast_in_dim.8, s32[256]{0:T(256)S(1)} %bitcast.24, s32[256]{0:T(256)S(1)} %get-tuple-element.2), kind=kCustom, calls=%fused_computation | custom fusion | bytes 5120 | tf_op jit(solution)/shard_map/scatter | solution.py:45
  20.5 0.7 copy.15
  21.2 16.6 %all-to-all-start = ((s32[128,1,4]{2,1,0:T(1,128)}), s32[128,1,4]{2,1,0:T(1,128)S(1)}, u32[]{:S(2)}, u32[]{:S(2)}) async-start(s32[128,1,4]{2,1,0:T(1,128)} %copy.15), calls=%async_computation | async-start | bytes 131072 | tf_op jit(solution)/shard_map/all_to_all | solution.py:56
  37.8 0.2 fusion.4
  38.0 15.6 %all_gather.3 = bf16[384,768]{1,0:T(8,128)(2,1)S(1)} all-gather(bf16[96,768]{1,0:T(8,128)(2,1)S(1)} %copy-done.1), channel_id=1, replica_groups=mesh['pts'=128,'lmk'=4] {'lmk'}, dimensions={0}, use_global_device_ids=true | all-gather | bytes 737280 | tf_op jit(solution)/shard_map/all_gather | solution.py:34
  53.6 0.2 fusion.1
  53.8 943.7 %all-reduce.2.cloned.1.call-done = bf16[384,512]{1,0:T(8,128)(2,1)} async-done(((bf16[384,512]{1,0:T(8,128)(2,1)}), bf16[384,512]{1,0:T(8,128)(2,1)}) %all-reduce.2.cloned.1.call-update) | async-done | bytes 393232 | tf_op jit(solution)/shard_map/psum | solution.py:13
  997.5 1.7 convolution_convert_fusion
  999.2 0.9 broadcast_in_dim.10
  1000.1 30.7 %scatter_fusion.1 = bf16[128,4,512]{2,1,0:T(4,128)(2,1)} fusion(bf16[128,4,512]{2,1,0:T(4,128)(2,1)} %broadcast_in_dim.10, s32[256]{0:T(256)S(1)} %bitcast.25, bf16[256,512]{1,0:T(8,128)(2,1)S(1)} %convolution_convert_fusion), kind=kCustom, calls=%fused_computation.1 | custom fusion | bytes 788480 | tf_op jit(solution)/shard_map/scatter | solution.py:52
  1030.9 7.7 all-to-all-start.1
  1038.5 0.5 broadcast.135
  1039.0 0.8 reduce.3
  1039.9 0.1 eq.48
  1040.0 0.6 convert_reduce_fusion
  1040.6 16.3 %all-to-all-done.1 = bf16[128,4,512]{2,1,0:T(4,128)(2,1)S(1)} async-done(((bf16[128,4,512]{2,1,0:T(4,128)(2,1)}), bf16[128,4,512]{2,1,0:T(4,128)(2,1)S(1)}, u32[]{:S(2)}, u32[]{:S(2)}) %all-to-all-start.1) | async-done | bytes 524320 | tf_op jit(solution)/shard_map/all_to_all | solution.py:55
  1056.9 0.1 reshape.67
  1057.0 0.8 convolution_multiply_fusion.1
  (20 shorter events, 0.1 us)
Async XLA Ops:
  7.2 990.3 %all-reduce.2.cloned.1.call-start = ((), (), s32[]{:S(2)}) async-start(), calls=%async_computation.2 | async-start | bytes 786432 | tf_op jit(solution)/shard_map/psum | solution.py:13
  7.9 0.8 copy-start.2
  9.4 28.5 %copy-start = (bf16[256,768]{1,0:T(8,128)(2,1)S(1)}, bf16[256,768]{1,0:T(8,128)(2,1)}, u32[]{:S(2)}) copy-start(bf16[256,768]{1,0:T(8,128)(2,1)} %param.5) | copy-start | bytes 1179652
  20.4 17.6 %copy-start.1 = (bf16[96,768]{1,0:T(8,128)(2,1)S(1)}, bf16[96,768]{1,0:T(8,128)(2,1)}, u32[]{:S(2)}) copy-start(bf16[96,768]{1,0:T(8,128)(2,1)} %param.6) | copy-start | bytes 442372
  21.2 1009.7 %all-to-all-start = ((s32[128,1,4]{2,1,0:T(1,128)}), s32[128,1,4]{2,1,0:T(1,128)S(1)}, u32[]{:S(2)}, u32[]{:S(2)}) async-start(s32[128,1,4]{2,1,0:T(1,128)} %copy.15), calls=%async_computation | async-start | bytes 131072 | tf_op jit(solution)/shard_map/all_to_all | solution.py:56
  1030.9 26.1 %all-to-all-start.1 = ((bf16[128,4,512]{2,1,0:T(4,128)(2,1)}), bf16[128,4,512]{2,1,0:T(4,128)(2,1)S(1)}, u32[]{:S(2)}, u32[]{:S(2)}) async-start(bf16[128,4,512]{2,1,0:T(4,128)(2,1)} %scatter_fusion.1), calls=%async_computation.1 | async-start | bytes 1048576 | tf_op jit(solution)/shard_map/all_to_all | solution.py:55
Sparse Core Ops, SparseCore 0:
  10.9 986.5 all-reduce.1
where the time goes:
time: 1070 us; the launch traced here: 1060 us
  waiting for transfers between devices  960 us (90%)
  local copies, waits for them, and re-layouts  44.4 us (4%)
  starting transfers between devices  24.3 us (2%)
  blocking collectives  15.6 us (1%)
  between operations  14.8 us (1%)
    psum x1, waiting for transfers between devices, spread(): return lax.psum(block, axis)  944 us
    scatter x1, local copies, waits for them, and re-layouts, body(): slots = jnp.zeros((point_groups, capacity, features.shape[1]), jnp.bfloat...  30.7 us
  transfers between devices with their start and end apart: 3, of which 2 were waited for; matrix products, arithmetic and copies ran while one was open for 5% of the time, Pallas kernels for 0%

commit v1 on v0

v1 whole, which is shorter than its diff:
```python
import functools
import math

import jax
import jax.numpy as jnp
from jax import lax
from jax.experimental import pallas as pl
from jax.experimental.pallas import tpu as pltpu
from jax.sharding import PartitionSpec as P

MESH = pl.DeviceIdType.MESH
CAP = 4
OWNED = 32
F32, BF16, I32 = jnp.float32, jnp.bfloat16, jnp.int32


def iota(shape, dim):
    return lax.broadcasted_iota(I32, shape, dim)


def dot(a, b, ca=1, cb=0):
    return lax.dot_general(a, b, (((ca,), (cb,)), ((), ())), preferred_element_type=F32)


def unit_rows(values):
    wide = values.astype(F32)
    scale = lax.rsqrt(jnp.mean(wide * wide, axis=1, keepdims=True) + 1e-06)
    return (wide * scale).astype(BF16)


def kernel(
    nx,
    nz,
    nl,
    index_ref,
    points_hbm,
    marks_hbm,
    panel_hbm,
    assign_hbm,
    out_ref,
    count_ref,
    points,
    marks,
    assign,
    slots,
    rows_z,
    regrouped,
    rows_q,
    pieces,
    planes,
    panel,
    sums,
    load_sem,
    rz_send,
    rz_recv,
    rq_send,
    rq_recv,
    p1_send,
    p1_recv,
    p2_send,
    p2_recv,
    p3_send,
    p3_recv,
    s_send,
    s_recv,
):
    nq = nx * 4
    me, my_l = lax.axis_index("pts"), lax.axis_index("lmk")
    my_x, my_z, my_yc = me // (nz * 4), (me // 4) % nz, me % 4
    my_y, my_c = my_yc // 2, my_yc % 2
    my_q = my_x * 4 + my_yc
    n_marks, depth = marks_hbm.shape
    n_points = points_hbm.shape[0]

    plane_peers = []
    for dx in range(nx):
        for dy in range(2):
            for dc in range(2):
                if dx or dy or dc:
                    x = (my_x + dx) % nx
                    yc = (my_y + dy) % 2 * 2 + (my_c + dc) % 2
                    plane_peers.append((x * 4 + yc, ((x * nz + my_z) * 4 + yc, my_l)))
    z_peers = []
    for dz in range(1, nz):
        z = (my_z + dz) % nz
        z_peers.append((z, ((my_x * nz + z) * 4 + my_yc, my_l)))
    l_peers = []
    for dl in range(1, nl):
        l = (my_l + dl) % nl
        l_peers.append((l, (me, l)))

    def piece_of(q):
        rows = pl.ds(pl.multiple_of(q // 4 * n_marks, n_marks), n_marks)
        return panel_hbm.at[0, rows, pl.ds(pl.multiple_of(q % 4 * 128, 128), 128)]

    loads = [
        pltpu.make_async_copy(points_hbm, points, load_sem.at[0]),
        pltpu.make_async_copy(marks_hbm, marks.at[pl.ds(0, n_marks)], load_sem.at[1]),
        pltpu.make_async_copy(assign_hbm, assign, load_sem.at[2]),
        pltpu.make_async_copy(piece_of(my_q), pieces.at[my_q], load_sem.at[3]),
    ]
    barrier = pltpu.get_barrier_semaphore()
    everyone = plane_peers + z_peers + l_peers
    for _, device in everyone:
        pl.semaphore_signal(barrier, inc=1, device_id=device, device_id_type=MESH)
    for load in loads:
        load.start()

    def remote(src, dst, send, recv, device):
        return pltpu.make_async_remote_copy(
            src_ref=src,
            dst_ref=dst,
            send_sem=send,
            recv_sem=recv,
            device_id=device,
            device_id_type=MESH,
        )

    marks[n_marks:, :] = jnp.zeros((128 - n_marks, depth), BF16)
    loads[2].wait()
    assigned = assign[...]
    owner, local = assigned // OWNED, assigned % OWNED
    n_owners = nq * nz
    hits = iota((n_owners, n_points), 0) == owner
    earlier = (iota((n_points, n_points), 0) < iota((n_points, n_points), 1)).astype(F32)
    before = dot(hits.astype(BF16), earlier.astype(BF16))
    rank = jnp.sum(jnp.where(hits, before, 0.0), axis=0, keepdims=True).astype(I32)
    owner_q = owner // (nz * 4) * 4 + owner % 4
    owner_z = owner // 4 % nz
    slot = (owner_z * nq + owner_q) * CAP + rank
    n_slots = n_owners * CAP
    to_slot = (iota((n_slots, n_points), 0) == slot).astype(F32).astype(BF16)
    local_hot = (iota((128, n_points), 0) == local + n_marks).astype(F32).astype(BF16)
    ids = dot(to_slot, local_hot, 1, 1)
    loads[0].wait()
    loads[1].wait()
    scores = dot(unit_rows(points[...]), unit_rows(marks[...]), 1, 1)
    rows = jnp.exp(scores * (0.5 / math.sqrt(depth)))
    rows = jnp.where(iota((n_points, 128), 1) < n_marks, rows, 0.0).astype(BF16)
    slots[...] = (dot(to_slot, rows) + ids).astype(BF16).reshape(nz, nq * CAP, 128)
    pl.semaphore_wait(barrier, len(everyone))

    p1 = [
        remote(piece_of(q), pieces.at[my_q], p1_send.at[q], p1_recv.at[my_q], device)
        for q, device in plane_peers
    ]
    rz = [
        remote(slots.at[z], rows_z.at[my_z], rz_send.at[z], rz_recv.at[my_z], device)
        for z, device in z_peers
    ]
    own = pltpu.make_async_copy(slots.at[my_z], rows_z.at[my_z], load_sem.at[4])
    for copy in rz + p1 + [own]:
        copy.start()

    source = index_ref[0]
    source_q = source // (nz * 4) * 4 + source % 4
    source_z = source // 4 % nz

    target = iota((n_slots, n_slots), 0)
    at_q, at_z, at_r = target // (nz * CAP), target // CAP % nz, target % CAP
    regroup = (iota((n_slots, n_slots), 1) == (at_z * nq + at_q) * CAP + at_r).astype(F32)
    regroup = regroup.astype(BF16)
    own.wait()
    for z, device in z_peers:
        remote(slots.at[z], rows_z.at[z], rz_send.at[z], rz_recv.at[z], device).wait_recv()
    grouped = dot(regroup, rows_z[...].reshape(n_slots, 128)).astype(BF16)
    regrouped[...] = grouped.reshape(nq, nz * CAP, 128)
    rq = [
        remote(regrouped.at[q], rows_q.at[my_q], rq_send.at[q], rq_recv.at[my_q], device)
        for q, device in plane_peers
    ]
    own = pltpu.make_async_copy(regrouped.at[my_q], rows_q.at[my_q], load_sem.at[4])
    for copy in rq + [own]:
        copy.start()

    loads[3].wait()
    for q, device in plane_peers:
        remote(piece_of(q), pieces.at[q], p1_send.at[q], p1_recv.at[q], device).wait_recv()
    planes[my_z] = pieces[source_q]
    p2 = [
        remote(planes.at[my_z], planes.at[my_z], p2_send.at[z], p2_recv.at[my_z], device)
        for z, device in z_peers
    ]
    for copy in p2:
        copy.start()

    own.wait()
    for q, device in plane_peers:
        remote(regrouped.at[q], rows_q.at[q], rq_send.at[q], rq_recv.at[q], device).wait_recv()
    received = rows_q[...].reshape(n_slots, 128)
    gram = dot(received, received, 0, 0)
    sums[my_l] = gram[n_marks:, :] * (OWNED * n_owners / (n_points * n_owners))
    s = [
        remote(sums.at[my_l], sums.at[my_l], s_send.at[l], s_recv.at[my_l], device)
        for l, device in l_peers
    ]
    for copy in s:
        copy.start()
    totals = dot(jnp.ones((8, n_slots), BF16), received)
    count_ref[...] = pltpu.roll(totals, 128 - n_marks, 1).astype(I32)

    for z, device in z_peers:
        remote(planes.at[z], planes.at[z], p2_send.at[z], p2_recv.at[z], device).wait_recv()
    panel[my_q] = planes[source_z]
    p3 = [
        remote(panel.at[my_q], panel.at[my_q], p3_send.at[q], p3_recv.at[my_q], device)
        for q, device in plane_peers
    ]
    for copy in p3:
        copy.start()

    for l, device in l_peers:
        remote(sums.at[l], sums.at[l], s_send.at[l], s_recv.at[l], device).wait_recv()
    factors = []
    for l in range(nl):
        whole = sums[l][:, :n_marks]
        high = whole.astype(BF16)
        factors.append(jnp.concatenate([high, (whole - high.astype(F32)).astype(BF16)], axis=0))
    for q, device in plane_peers:
        remote(panel.at[q], panel.at[q], p3_send.at[q], p3_recv.at[q], device).wait_recv()
    for column in range(4):
        both = dot(factors[0], panel[column])
        for l in range(1, nl):
            both = both + dot(factors[l], panel[l * 4 + column])
        out_ref[:, column * 128 : (column + 1) * 128] = both[:OWNED] + both[OWNED:]
    for copy in rz + p1 + rq + p2 + s + p3:
        copy.wait_send()


def solution(mesh):
    pts, nl = mesh.shape["pts"], mesh.shape["lmk"]
    nx = nl
    nz = pts // (nx * 4)
    nq = nx * 4

    def body(points, landmarks, panels, panel_index, assignment):
        n_points, depth = points.shape
        n_marks = landmarks.shape[0]
        columns = panels.shape[2]
        hbm = pl.BlockSpec(memory_space=pl.ANY)
        vmem = pl.BlockSpec(memory_space=pltpu.VMEM)
        dma = pltpu.SemaphoreType.DMA
        out, counts = pl.pallas_call(
            functools.partial(kernel, nx, nz, nl),
            out_shape=(
                jax.ShapeDtypeStruct((OWNED, columns), F32),
                jax.ShapeDtypeStruct((8, 128), I32),
            ),
            in_specs=[pl.BlockSpec(memory_space=pltpu.SMEM), hbm, hbm, hbm, hbm],
            out_specs=(vmem, vmem),
            scratch_shapes=[
                pltpu.VMEM((n_points, depth), BF16),
                pltpu.VMEM((128, depth), BF16),
                pltpu.VMEM((1, n_points), I32),
                pltpu.VMEM((nz, nq * CAP, 128), BF16),
                pltpu.VMEM((nz, nq * CAP, 128), BF16),
                pltpu.VMEM((nq, nz * CAP, 128), BF16),
                pltpu.VMEM((nq, nz * CAP, 128), BF16),
                pltpu.VMEM((nq, n_marks, 128), BF16),
                pltpu.VMEM((nz, n_marks, 128), BF16),
                pltpu.VMEM((nq, n_marks, 128), BF16),
                pltpu.VMEM((nl, OWNED, 128), F32),
                dma((5,)),
                dma((nz,)),
                dma((nz,)),
                dma((nq,)),
                dma((nq,)),
                dma((nq,)),
                dma((nq,)),
                dma((nz,)),
                dma((nz,)),
                dma((nq,)),
                dma((nq,)),
                dma((nl,)),
                dma((nl,)),
            ],
            compiler_params=pltpu.CompilerParams(collective_id=0, has_side_effects=True),
        )(panel_index, points, landmarks, panels, assignment.reshape(1, n_points))
        return out, counts[0, :OWNED]

    in_specs = (P("pts", None), P("lmk", None), P("pts", None, "lmk"), P(), P("pts"))
    out_specs = (P("pts", "lmk"), P("pts"))
    return jax.shard_map(body, mesh=mesh, in_specs=in_specs, out_specs=out_specs, check_vma=False)
```

time: 1070 us -> 42.3 us (0.04)
  waiting for transfers between devices: 960 us -> 0 us
  local copies, waits for them, and re-layouts: 44.4 us -> 2.66 us
  Pallas kernels: 0 us -> 38.1 us
  starting transfers between devices: 24.3 us -> 0 us
  blocking collectives: 15.6 us -> 0 us
  between operations: 14.8 us -> 1.29 us
    psum x1 -> x0, waiting for transfers between devices: 944 us -> none  [spread(): return lax.psum(block, axis)]
    scatter x2 -> x0, local copies, waits for them, and re-layouts: 41.8 us -> none  [the longest x1 30.7 us: body(): slots = jnp.zeros((point_groups, capacity, features.shape[1]), jnp.bfloat...]
    pallas_call x0 -> x1, Pallas kernels: none -> 38.1 us  [body(): pl.pallas_call(functools.partial(kernel, nx, nz, nl), out_shape=(jax.Shap...]
    all_to_all x2 -> x0, starting transfers between devices: 24.3 us -> none  [the longest x1 16.6 us: body(): lax.all_to_all(slot_ids, 'pts', split_axis=0, concat_axis=0, tiled=True)]
    all_to_all x2 -> x0, waiting for transfers between devices: 16.3 us -> none  [the longest x1 16.3 us: body(): lax.all_to_all(slots, 'pts', split_axis=0, concat_axis=0, tiled=True)]
    all_gather x1 -> x0, blocking collectives: 15.6 us -> none  [body(): lax.all_gather(landmarks, 'lmk', axis=0, tiled=True)]
  transfers between devices with their start and end apart: 3 -> 0, of which waited for: 2 -> 0; matrix products, arithmetic and copies ran while one was open for 5% -> 0% of each run, Pallas kernels for 0% -> 0%
where the time goes in v1:
time: 42.3 us; the launch traced here: 42.1 us
  Pallas kernels  38.1 us (90%)
  local copies, waits for them, and re-layouts  2.66 us (6%)
  between operations  1.29 us (3%)
    pallas_call x1, Pallas kernels, body(): pl.pallas_call(functools.partial(kernel, nx, nz, nl), out_shape=(jax.Shap...  38.1 us
    unnamed x1, local copies, waits for them, and re-layouts  1.47 us
    squeeze x1, local copies, waits for them, and re-layouts, body(): return (out, counts[0, :OWNED])  1.19 us

profile of v1, /device:TPU:1, one launch (start us, length us, event | category | flops | bytes accessed | tf_op | source)
XLA Modules:
  0.0 42.1 jit_solution(12568176101942986746)
XLA Ops:
  1.3 38.1 %shard_map.68 = (f32[32,512]{1,0:T(8,128)}, s32[8,128]{1,0:T(8,128)}) custom-call(s32[1]{0:T(128)S(6)} %copy.8.index_ref, bf16[256,768]{1,0:T(8,128)(2,1)} %points_hbm.1, bf16[96,768]{1,0:T(8,128)(2,1)} %marks_hbm.1, bf16[1,384,512]{2,1,0:T(8,128)(2,1)} %panel_hbm.1, s32[1,256]{1,0:T(1,128)} %bitcast.3), custom_call_target="tpu_custom_call" | custom-call | tf_op jit(solution)/shard_map/pallas_call | solution.py:243
  39.4 1.2 %slice_bitcast_fusion = s32[32]{0:T(128)} fusion(s32[8,128]{1,0:T(8,128)} %get-tuple-element.5), kind=kLoop, calls=%fused_computation | loop fusion | bytes 256 | tf_op jit(solution)/shard_map/squeeze | solution.py:279
  40.6 1.5 %copy.9 = f32[32,512]{1,0:T(8,128)} copy(f32[32,512]{1,0:T(8,128)} %get-tuple-element.8) | data formatting | bytes 131072

commit v2 on v1

v2 whole, which is shorter than its diff:
```python
import functools
import math

import jax
import jax.numpy as jnp
from jax import lax
from jax.experimental import pallas as pl
from jax.experimental.pallas import tpu as pltpu
from jax.sharding import PartitionSpec as P

MESH = pl.DeviceIdType.MESH
CAP = 4
CHUNKS = 2
OWNED = 32
F32, BF16, I32 = jnp.float32, jnp.bfloat16, jnp.int32


def iota(shape, dim):
    return lax.broadcasted_iota(I32, shape, dim)


def dot(a, b, ca=1, cb=0):
    return lax.dot_general(a, b, (((ca,), (cb,)), ((), ())), preferred_element_type=F32)


def unit_rows(values):
    wide = values.astype(F32)
    scale = lax.rsqrt(jnp.mean(wide * wide, axis=1, keepdims=True) + 1e-06)
    return (wide * scale).astype(BF16)


def kernel(
    nx,
    nz,
    nl,
    index_hbm,
    points_hbm,
    marks_hbm,
    panel_hbm,
    assign_hbm,
    out_ref,
    count_ref,
    index_ref,
    points,
    marks,
    assign,
    mine,
    slots,
    rows_z,
    regrouped,
    rows_q,
    pieces,
    planes,
    panel,
    sums,
    load_sem,
    rz_send,
    rz_recv,
    rq_send,
    rq_recv,
    p1_send,
    p1_recv,
    p2_send,
    p2_recv,
    p3_send,
    p3_recv,
    s_send,
    s_recv,
):
    nq = nx * 4
    me, my_l = lax.axis_index("pts"), lax.axis_index("lmk")
    my_x, my_z, my_yc = me // (nz * 4), (me // 4) % nz, me % 4
    my_y, my_c = my_yc // 2, my_yc % 2
    my_q = my_x * 4 + my_yc
    n_marks, depth = marks_hbm.shape
    n_points = points_hbm.shape[0]

    plane_peers = []
    for dx in range(nx):
        for dy in range(2):
            for dc in range(2):
                if dx or dy or dc:
                    x = (my_x + dx) % nx
                    yc = (my_y + dy) % 2 * 2 + (my_c + dc) % 2
                    plane_peers.append((x * 4 + yc, ((x * nz + my_z) * 4 + yc, my_l)))
    z_peers = []
    for dz in range(1, nz):
        z = (my_z + dz) % nz
        z_peers.append((z, ((my_x * nz + z) * 4 + my_yc, my_l)))
    l_peers = []
    for dl in range(1, nl):
        l = (my_l + dl) % nl
        l_peers.append((l, (me, l)))

    step = n_marks // CHUNKS
    chunks = [pl.ds(k * step, step) for k in range(CHUNKS)]

    def chunk_at(ref, q, k):
        rows = pl.ds(pl.multiple_of(q // 4 * n_marks + k * step, step), step)
        return ref.at[rows, pl.ds(pl.multiple_of(q % 4 * 128, 128), 128)]

    loads = [
        pltpu.make_async_copy(points_hbm, points, load_sem.at[0]),
        pltpu.make_async_copy(marks_hbm, marks.at[pl.ds(0, n_marks)], load_sem.at[1]),
        pltpu.make_async_copy(assign_hbm, assign, load_sem.at[2]),
                pltpu.make_async_copy(panel_hbm.at[0], mine, load_sem.at[3]),
        pltpu.make_async_copy(index_hbm, index_ref, load_sem.at[5]),
    ]
    loads += [
        pltpu.make_async_copy(chunk_at(panel_hbm.at[0], my_q, k), pieces[k].at[my_q], load_sem.at[6 + k])
        for k in range(CHUNKS)
    ]
    barrier = pltpu.get_barrier_semaphore()
    everyone = z_peers + l_peers + plane_peers
    for _, device in everyone:
        pl.semaphore_signal(barrier, inc=1, device_id=device, device_id_type=MESH)
    for load in loads:
        load.start()

    def remote(src, dst, send, recv, device):
        return pltpu.make_async_remote_copy(
            src_ref=src,
            dst_ref=dst,
            send_sem=send,
            recv_sem=recv,
            device_id=device,
            device_id_type=MESH,
        )

    marks[n_marks:, :] = jnp.zeros((128 - n_marks, depth), BF16)
    loads[2].wait()
    assigned = assign[...]
    owner, local = assigned // OWNED, assigned % OWNED
    n_owners = nq * nz
    hits = iota((n_owners, n_points), 0) == owner
    earlier = (iota((n_points, n_points), 0) < iota((n_points, n_points), 1)).astype(F32)
    before = dot(hits.astype(BF16), earlier.astype(BF16))
    rank = jnp.sum(jnp.where(hits, before, 0.0), axis=0, keepdims=True).astype(I32)
    owner_q = owner // (nz * 4) * 4 + owner % 4
    owner_z = owner // 4 % nz
    slot = (owner_z * nq + owner_q) * CAP + rank
    n_slots = n_owners * CAP
    to_slot = (iota((n_slots, n_points), 0) == slot).astype(F32).astype(BF16)
    local_hot = (iota((128, n_points), 0) == local + n_marks).astype(F32).astype(BF16)
    ids = dot(to_slot, local_hot, 1, 1)
    loads[0].wait()
    loads[1].wait()
    scores = dot(unit_rows(points[...]), unit_rows(marks[...]), 1, 1)
    rows = jnp.exp(scores * (0.5 / math.sqrt(depth)))
    rows = jnp.where(iota((n_points, 128), 1) < n_marks, rows, 0.0).astype(BF16)
    slots[...] = (dot(to_slot, rows) + ids).astype(BF16).reshape(nz, nq * CAP, 128)
    pl.semaphore_wait(barrier, len(everyone))

    sent = []

    def start(copies):
        for copy in copies:
            copy.start()
        sent.extend(copies)

    def scatter_copies(k):
        out, back = [], []
        for q, device in plane_peers:
            src, send, recv, dst = chunk_at(mine, q, k), p1_send.at[k, q], p1_recv, pieces[k]
            out.append(remote(src, dst.at[my_q], send, recv.at[k, my_q], device))
            back.append(remote(src, dst.at[q], send, recv.at[k, q], device))
        return out, back

    def gather_copies(k):
        out, back = [], []
        for q, device in plane_peers:
            here, there, send = panel.at[my_q, chunks[k]], panel.at[q, chunks[k]], p3_send.at[k, q]
            out.append(remote(here, here, send, p3_recv.at[k, my_q], device))
            back.append(remote(there, there, send, p3_recv.at[k, q], device))
        return out, back

    def z_copies(k):
        out, back = [], []
        for z, device in z_peers:
            here, there, send = planes[k].at[my_z], planes[k].at[z], p2_send.at[k, z]
            out.append(remote(here, here, send, p2_recv.at[k, my_z], device))
            back.append(remote(there, there, send, p2_recv.at[k, z], device))
        return out, back

    def arrive(copies):
        for copy in copies:
            copy.wait_recv()

    rz, rz_back, rq, rq_back, s, s_back = [], [], [], [], [], []
    for z, device in z_peers:
        rz.append(remote(slots.at[z], rows_z.at[my_z], rz_send.at[z], rz_recv.at[my_z], device))
        rz_back.append(remote(slots.at[z], rows_z.at[z], rz_send.at[z], rz_recv.at[z], device))
    for q, device in plane_peers:
        rq.append(remote(regrouped.at[q], rows_q.at[my_q], rq_send.at[q], rq_recv.at[my_q], device))
        rq_back.append(remote(regrouped.at[q], rows_q.at[q], rq_send.at[q], rq_recv.at[q], device))
    for l, device in l_peers:
        s.append(remote(sums.at[my_l], sums.at[my_l], s_send.at[l], s_recv.at[my_l], device))
        s_back.append(remote(sums.at[l], sums.at[l], s_send.at[l], s_recv.at[l], device))
    own_z = pltpu.make_async_copy(slots.at[my_z], rows_z.at[my_z], load_sem.at[4])
    own_q = pltpu.make_async_copy(regrouped.at[my_q], rows_q.at[my_q], load_sem.at[4])
    p1 = [scatter_copies(k) for k in range(CHUNKS)]
    p2 = [z_copies(k) for k in range(CHUNKS)]
    p3 = [gather_copies(k) for k in range(CHUNKS)]

    def scatter(k):
        if k == 0:
            loads[3].wait()
        start(p1[k][0])

    def source():
        holder = index_ref[0, 0]
        return holder // (nz * 4) * 4 + holder % 4, holder // 4 % nz

    def along_z(k):
        if k == 0:
            loads[4].wait()
        loads[5 + k].wait()
        arrive(p1[k][1])
        planes[k][my_z] = pieces[k][source()[0]]
        start(p2[k][0])

    def gather(k):
        arrive(p2[k][1])
        panel[my_q, chunks[k]] = planes[k][source()[1]]
        start(p3[k][0])

    def rows_along_z():
        start(rz)
        own_z.start()

    def rows_in_plane():
        target = iota((n_slots, n_slots), 0)
        at_q, at_z, at_r = target // (nz * CAP), target // CAP % nz, target % CAP
        regroup = iota((n_slots, n_slots), 1) == (at_z * nq + at_q) * CAP + at_r
        regroup = regroup.astype(F32).astype(BF16)
        own_z.wait()
        arrive(rz_back)
        grouped = dot(regroup, rows_z[...].reshape(n_slots, 128)).astype(BF16)
        regrouped[...] = grouped.reshape(nq, nz * CAP, 128)
        start(rq)
        own_q.start()

    def sum_rows():
        own_q.wait()
        arrive(rq_back)
        received = rows_q[...].reshape(n_slots, 128)
        gram = dot(received, received, 0, 0)
        sums[my_l] = gram[n_marks:, :] * (OWNED * n_owners / (n_points * n_owners))
        start(s)
        totals = dot(jnp.ones((8, n_slots), BF16), received)
        count_ref[...] = pltpu.roll(totals, 128 - n_marks, 1)[:1, :OWNED].astype(I32)

    def finish():
        arrive(s_back)
        factors = []
        for l in range(nl):
            whole = sums[l][:, :n_marks]
            high = whole.astype(BF16)
            low = (whole - high.astype(F32)).astype(BF16)
            factors.append(jnp.concatenate([high, low], axis=0))
        for k in range(CHUNKS):
            arrive(p3[k][1])
        for column in range(4):
            both = dot(factors[0], panel[column])
            for l in range(1, nl):
                both = both + dot(factors[l], panel[l * 4 + column])
            out_ref[:, column * 128 : (column + 1) * 128] = both[:OWNED] + both[OWNED:]

    scatter(0)
    rows_along_z()
    for k in range(1, CHUNKS):
        scatter(k)
    along_z(0)
    rows_in_plane()
    for k in range(1, CHUNKS):
        along_z(k)
    gather(0)
    sum_rows()
    for k in range(1, CHUNKS):
        gather(k)
    finish()

    for copy in sent:
        copy.wait_send()


def write_out(total, count, out_hbm, count_hbm, sems):
    copies = [
        pltpu.make_async_copy(total, out_hbm, sems.at[0]),
        pltpu.make_async_copy(count, count_hbm, sems.at[1]),
    ]
    for copy in copies:
        copy.start()
    for copy in copies:
        copy.wait()


def solution(mesh):
    pts, nl = mesh.shape["pts"], mesh.shape["lmk"]
    nx = nl
    nz = pts // (nx * 4)
    nq = nx * 4

    def body(points, landmarks, panels, panel_index, assignment):
        n_points, depth = points.shape
        n_marks = landmarks.shape[0]
        columns = panels.shape[2]
        hbm = pl.BlockSpec(memory_space=pl.ANY)
        vmem = pl.BlockSpec(memory_space=pltpu.VMEM)
        dma = pltpu.SemaphoreType.DMA
        out, counts = pl.pallas_call(
            functools.partial(kernel, nx, nz, nl),
            out_shape=(
                pltpu.VMEM((OWNED, columns), F32),
                pltpu.VMEM((1, OWNED), I32),
            ),
            in_specs=[hbm] * 5,
            out_specs=(vmem, vmem),
            scratch_shapes=[
                pltpu.SMEM((1, 1), I32),
                pltpu.VMEM((n_points, depth), BF16),
                pltpu.VMEM((128, depth), BF16),
                pltpu.VMEM((1, n_points), I32),
                pltpu.VMEM((nl * n_marks, columns), BF16),
                pltpu.VMEM((nz, nq * CAP, 128), BF16),
                pltpu.VMEM((nz, nq * CAP, 128), BF16),
                pltpu.VMEM((nq, nz * CAP, 128), BF16),
                pltpu.VMEM((nq, nz * CAP, 128), BF16),
                [pltpu.VMEM((nq, n_marks // CHUNKS, 128), BF16)] * CHUNKS,
                [pltpu.VMEM((nz, n_marks // CHUNKS, 128), BF16)] * CHUNKS,
                pltpu.VMEM((nq, n_marks, 128), BF16),
                pltpu.VMEM((nl, OWNED, 128), F32),
                dma((6 + CHUNKS,)),
                dma((nz,)),
                dma((nz,)),
                dma((nq,)),
                dma((nq,)),
                dma((CHUNKS, nq)),
                dma((CHUNKS, nq)),
                dma((CHUNKS, nz)),
                dma((CHUNKS, nz)),
                dma((CHUNKS, nq)),
                dma((CHUNKS, nq)),
                dma((nl,)),
                dma((nl,)),
            ],
            compiler_params=pltpu.CompilerParams(collective_id=0, has_side_effects=True),
        )(panel_index.reshape(1, 1), points, landmarks, panels, assignment.reshape(1, n_points))
        out, counts = pl.pallas_call(
            write_out,
            out_shape=(
                jax.ShapeDtypeStruct((OWNED, columns), F32),
                jax.ShapeDtypeStruct((1, OWNED), I32),
            ),
            in_specs=[vmem, vmem],
            out_specs=(hbm, hbm),
            scratch_shapes=[dma((2,))],
        )(*(pltpu.with_memory_space_constraint(a, pltpu.VMEM) for a in (out, counts)))
        return out, counts.reshape(OWNED)

    in_specs = (P("pts", None), P("lmk", None), P("pts", None, "lmk"), P(), P("pts"))
    out_specs = (P("pts", "lmk"), P("pts"))
    return jax.shard_map(body, mesh=mesh, in_specs=in_specs, out_specs=out_specs, check_vma=False)
```

time: 42.3 us -> 38.6 us (0.913)
  local copies, waits for them, and re-layouts: 2.66 us -> 0 us
  Pallas kernels: 38.1 us -> 37.1 us
    unnamed x1 -> x0, local copies, waits for them, and re-layouts: 1.47 us -> none
    squeeze x1 -> x0, local copies, waits for them, and re-layouts: 1.19 us -> none  [body(): return (out, counts[0, :OWNED])]
    pallas_call x1 -> x2, Pallas kernels: 38.1 us -> 37.1 us  [the longest x1 36.5 us: body(): pl.pallas_call(functools.partial(kernel, nx, nz, nl), out_shape=(pltpu.VM...]
where the time goes in v2:
time: 38.6 us; the launch traced here: 38.4 us
  Pallas kernels  37.1 us (96%)
  between operations  1.28 us (3%)
    pallas_call x1, Pallas kernels, body(): pl.pallas_call(functools.partial(kernel, nx, nz, nl), out_shape=(pltpu.VM...  36.5 us

profile of v2, /device:TPU:1, one launch (start us, length us, event | category | flops | bytes accessed | tf_op | source)
XLA Modules:
  0.0 38.4 jit_solution(6787192946841944042)
XLA Ops:
  1.3 36.5 %shard_map.68 = (f32[32,512]{1,0:T(8,128)S(1)}, s32[1,32]{1,0:T(1,128)S(1)}) custom-call(s32[1,1]{1,0:T(1,128)} %bitcast.3.index_hbm, bf16[256,768]{1,0:T(8,128)(2,1)} %points_hbm.1, bf16[96,768]{1,0:T(8,128)(2,1)} %marks_hbm.1, bf16[1,384,512]{2,1,0:T(8,128)(2,1)} %panel_hbm.1, s32[1,256]{1,0:T(1,128)} %bitcast.4), custom_call_target="tpu_custom_call" | custom-call | tf_op jit(solution)/shard_map/pallas_call | solution.py:311
  37.8 0.7 %shard_map.69 = (f32[32,512]{1,0:T(8,128)}, s32[1,32]{1,0:T(1,128)}) custom-call(f32[32,512]{1,0:T(8,128)S(1)} %get-tuple-element.6.total, s32[1,32]{1,0:T(1,128)S(1)} %get-tuple-element.7.count), custom_call_target="tpu_custom_call" | custom-call | tf_op jit(solution)/shard_map/pallas_call | solution.py:349

commit v3 on v2

--- a/solution.py
+++ b/solution.py
@@ -10,7 +10,7 @@
 
 MESH = pl.DeviceIdType.MESH
 CAP = 4
-CHUNKS = 2
+CHUNKS = 3
 OWNED = 32
 F32, BF16, I32 = jnp.float32, jnp.bfloat16, jnp.int32
 
@@ -45,6 +45,8 @@
     marks,
     assign,
     mine,
+    halves,
+    chosen,
     slots,
     rows_z,
     regrouped,
@@ -58,14 +60,20 @@
     rz_recv,
     rq_send,
     rq_recv,
+    c1_send,
+    c1_recv,
     p1_send,
     p1_recv,
     p2_send,
     p2_recv,
     p3_send,
     p3_recv,
+    c3_send,
+    c3_recv,
     s_send,
     s_recv,
+    in_z,
+    in_l,
 ):
     nq = nx * 4
     me, my_l = lax.axis_index("pts"), lax.axis_index("lmk")
@@ -83,8 +91,17 @@
                     x = (my_x + dx) % nx
                     yc = (my_y + dy) % 2 * 2 + (my_c + dc) % 2
                     plane_peers.append((x * 4 + yc, ((x * nz + my_z) * 4 + yc, my_l)))
+    other_c = 1 - my_c
+    sibling = (me + other_c - my_c, my_l)
+    my_xy = my_x * 2 + my_y
+    xy_peers = []
+    for dx in range(nx):
+        for dy in range(2):
+            if dx or dy:
+                x, y = (my_x + dx) % nx, (my_y + dy) % 2
+                xy_peers.append((x, y, ((x * nz + my_z) * 4 + y * 2 + my_c, my_l)))
     z_peers = []
-    for dz in range(1, nz):
+    for dz in range(nz - 1, 0, -1):
         z = (my_z + dz) % nz
         z_peers.append((z, ((my_x * nz + z) * 4 + my_yc, my_l)))
     l_peers = []
@@ -95,25 +112,34 @@
     step = n_marks // CHUNKS
     chunks = [pl.ds(k * step, step) for k in range(CHUNKS)]
 
-    def chunk_at(ref, q, k):
-        rows = pl.ds(pl.multiple_of(q // 4 * n_marks + k * step, step), step)
-        return ref.at[rows, pl.ds(pl.multiple_of(q % 4 * 128, 128), 128)]
+    def half_of(ref, y, c, k):
+        return ref.at[:, chunks[k], pl.ds(pl.multiple_of((y * 2 + c) * 128, 128), 128)]
 
     loads = [
         pltpu.make_async_copy(points_hbm, points, load_sem.at[0]),
         pltpu.make_async_copy(marks_hbm, marks.at[pl.ds(0, n_marks)], load_sem.at[1]),
         pltpu.make_async_copy(assign_hbm, assign, load_sem.at[2]),
-                pltpu.make_async_copy(panel_hbm.at[0], mine, load_sem.at[3]),
+                pltpu.make_async_copy(panel_hbm, mine, load_sem.at[3]),
         pltpu.make_async_copy(index_hbm, index_ref, load_sem.at[5]),
     ]
     loads += [
-        pltpu.make_async_copy(chunk_at(panel_hbm.at[0], my_q, k), pieces[k].at[my_q], load_sem.at[6 + k])
+        pltpu.make_async_copy(
+            half_of(panel_hbm, y, my_c, k), halves[k].at[my_c, y], load_sem.at[6 + 2 * k + y]
+        )
         for k in range(CHUNKS)
+        for y in range(2)
     ]
     barrier = pltpu.get_barrier_semaphore()
-    everyone = z_peers + l_peers + plane_peers
-    for _, device in everyone:
-        pl.semaphore_signal(barrier, inc=1, device_id=device, device_id_type=MESH)
+
+    def signal(semaphore, device):
+        pl.semaphore_signal(semaphore, inc=1, device_id=device, device_id_type=MESH)
+
+    for z, device in z_peers:
+        pl.when(z > my_z)(functools.partial(signal, barrier, device))
+    for _, device in plane_peers:
+        signal(barrier, device)
+    for l, device in l_peers:
+        pl.when(l > my_l)(functools.partial(signal, barrier, device))
     for load in loads:
         load.start()
 
@@ -127,29 +153,43 @@
             device_id_type=MESH,
         )
 
-    marks[n_marks:, :] = jnp.zeros((128 - n_marks, depth), BF16)
-    loads[2].wait()
-    assigned = assign[...]
-    owner, local = assigned // OWNED, assigned % OWNED
     n_owners = nq * nz
-    hits = iota((n_owners, n_points), 0) == owner
-    earlier = (iota((n_points, n_points), 0) < iota((n_points, n_points), 1)).astype(F32)
-    before = dot(hits.astype(BF16), earlier.astype(BF16))
-    rank = jnp.sum(jnp.where(hits, before, 0.0), axis=0, keepdims=True).astype(I32)
-    owner_q = owner // (nz * 4) * 4 + owner % 4
-    owner_z = owner // 4 % nz
-    slot = (owner_z * nq + owner_q) * CAP + rank
     n_slots = n_owners * CAP
-    to_slot = (iota((n_slots, n_points), 0) == slot).astype(F32).astype(BF16)
-    local_hot = (iota((128, n_points), 0) == local + n_marks).astype(F32).astype(BF16)
-    ids = dot(to_slot, local_hot, 1, 1)
-    loads[0].wait()
-    loads[1].wait()
-    scores = dot(unit_rows(points[...]), unit_rows(marks[...]), 1, 1)
-    rows = jnp.exp(scores * (0.5 / math.sqrt(depth)))
-    rows = jnp.where(iota((n_points, 128), 1) < n_marks, rows, 0.0).astype(BF16)
-    slots[...] = (dot(to_slot, rows) + ids).astype(BF16).reshape(nz, nq * CAP, 128)
-    pl.semaphore_wait(barrier, len(everyone))
+    made = {}
+
+    def assign_slots():
+        marks[n_marks:, :] = jnp.zeros((128 - n_marks, depth), BF16)
+        loads[2].wait()
+        assigned = assign[...]
+        owner, local = assigned // OWNED, assigned % OWNED
+        hits = iota((n_owners, n_points), 0) == owner
+        earlier = (iota((n_points, n_points), 0) < iota((n_points, n_points), 1)).astype(F32)
+        before = dot(hits.astype(BF16), earlier.astype(BF16))
+        rank = jnp.sum(jnp.where(hits, before, 0.0), axis=0, keepdims=True).astype(I32)
+        owner_q = owner // (nz * 4) * 4 + owner % 4
+        owner_z = owner // 4 % nz
+        slot = (owner_z * nq + owner_q) * CAP + rank
+        to_slot = (iota((n_slots, n_points), 0) == slot).astype(F32).astype(BF16)
+        local_hot = (iota((128, n_points), 0) == local + n_marks).astype(F32).astype(BF16)
+        made["to_slot"], made["ids"] = to_slot, dot(to_slot, local_hot, 1, 1)
+
+    def kernel_rows():
+        loads[0].wait()
+        loads[1].wait()
+        scores = dot(unit_rows(points[...]), unit_rows(marks[...]), 1, 1)
+        rows = jnp.exp(scores * (0.5 / math.sqrt(depth)))
+        made["rows"] = jnp.where(iota((n_points, 128), 1) < n_marks, rows, 0.0).astype(BF16)
+
+    def fill_slots():
+        filled = dot(made["to_slot"], made["rows"]) + made["ids"]
+        slots[...] = filled.astype(BF16).reshape(nz, nq * CAP, 128)
+
+    def everyone_in():
+        pl.semaphore_wait(barrier, len(plane_peers) + my_z + my_l)
+        for z, device in z_peers:
+            pl.when(z < my_z)(functools.partial(signal, in_z.at[my_z], device))
+        for l, device in l_peers:
+            pl.when(l < my_l)(functools.partial(signal, in_l.at[my_l], device))
 
     sent = []
 
@@ -158,21 +198,36 @@
             copy.start()
         sent.extend(copies)
 
+    def core_copies(k):
+        out, back = [], []
+        for y in range(2):
+            src, send, recv = half_of(mine, y, other_c, k), c1_send.at[k, y], c1_recv.at[k, y]
+            out.append(remote(src, halves[k].at[my_c, y], send, recv, sibling))
+            back.append(remote(src, halves[k].at[other_c, y], send, recv, sibling))
+        return out, back
+
     def scatter_copies(k):
         out, back = [], []
-        for q, device in plane_peers:
-            src, send, recv, dst = chunk_at(mine, q, k), p1_send.at[k, q], p1_recv, pieces[k]
-            out.append(remote(src, dst.at[my_q], send, recv.at[k, my_q], device))
-            back.append(remote(src, dst.at[q], send, recv.at[k, q], device))
+        for x, y, device in xy_peers:
+            src, at, dst = chosen[k].at[y, x], x * 2 + y, pieces[k]
+            out.append(remote(src, dst.at[my_xy], p1_send.at[k, at], p1_recv.at[k, my_xy], device))
+            back.append(remote(src, dst.at[at], p1_send.at[k, at], p1_recv.at[k, at], device))
         return out, back
 
     def gather_copies(k):
         out, back = [], []
-        for q, device in plane_peers:
-            here, there, send = panel.at[my_q, chunks[k]], panel.at[q, chunks[k]], p3_send.at[k, q]
-            out.append(remote(here, here, send, p3_recv.at[k, my_q], device))
-            back.append(remote(there, there, send, p3_recv.at[k, q], device))
+        here = panel.at[my_c, my_xy, chunks[k]]
+        for x, y, device in xy_peers:
+            at = x * 2 + y
+            there = panel.at[my_c, at, chunks[k]]
+            out.append(remote(here, here, p3_send.at[k, at], p3_recv.at[k, my_xy], device))
+            back.append(remote(there, there, p3_send.at[k, at], p3_recv.at[k, at], device))
         return out, back
+
+    def share_copies(k):
+        here, there = panel.at[my_c, :, chunks[k]], panel.at[other_c, :, chunks[k]]
+        out = remote(here, here, c3_send.at[k], c3_recv.at[k], sibling)
+        return [out], [remote(there, there, c3_send.at[k], c3_recv.at[k], sibling)]
 
     def z_copies(k):
         out, back = [], []
@@ -198,35 +253,60 @@
         s_back.append(remote(sums.at[l], sums.at[l], s_send.at[l], s_recv.at[l], device))
     own_z = pltpu.make_async_copy(slots.at[my_z], rows_z.at[my_z], load_sem.at[4])
     own_q = pltpu.make_async_copy(regrouped.at[my_q], rows_q.at[my_q], load_sem.at[4])
+    c1 = [core_copies(k) for k in range(CHUNKS)]
     p1 = [scatter_copies(k) for k in range(CHUNKS)]
     p2 = [z_copies(k) for k in range(CHUNKS)]
     p3 = [gather_copies(k) for k in range(CHUNKS)]
+    c3 = [share_copies(k) for k in range(CHUNKS)]
+
+    def to_sibling(k):
+        if k == 0:
+            loads[3].wait()
+        start(c1[k][0])
+
+    def source():
+        holder = index_ref[0, 0]
+        yc = holder % 4
+        return yc % 2, holder // (nz * 4) * 2 + yc // 2, holder // 4 % nz
 
     def scatter(k):
         if k == 0:
-            loads[3].wait()
+            loads[4].wait()
+        for y in range(2):
+            loads[5 + 2 * k + y].wait()
+        arrive(c1[k][1])
+        chosen[k][...] = halves[k][source()[0]]
+        pieces[k][my_xy] = chosen[k][my_y, my_x]
         start(p1[k][0])
 
-    def source():
-        holder = index_ref[0, 0]
-        return holder // (nz * 4) * 4 + holder % 4, holder // 4 % nz
-
     def along_z(k):
-        if k == 0:
-            loads[4].wait()
-        loads[5 + k].wait()
         arrive(p1[k][1])
-        planes[k][my_z] = pieces[k][source()[0]]
+        planes[k][my_z] = pieces[k][source()[1]]
         start(p2[k][0])
 
     def gather(k):
         arrive(p2[k][1])
-        panel[my_q, chunks[k]] = planes[k][source()[1]]
+        panel[my_c, my_xy, chunks[k]] = planes[k][source()[2]]
         start(p3[k][0])
 
-    def rows_along_z():
-        start(rz)
+    def share(k):
+        arrive(p3[k][1])
+        start(c3[k][0])
+
+    def rows_down():
         own_z.start()
+        for (z, _), copy in zip(z_peers, rz):
+            pl.when(z < my_z)(copy.start)
+
+    def rows_up():
+        for (z, _), copy in zip(z_peers, rz):
+
+            @pl.when(z > my_z)
+            def _():
+                pl.semaphore_wait(in_z.at[z], 1)
+                copy.start()
+
+        sent.extend(rz)
 
     def rows_in_plane():
         target = iota((n_slots, n_slots), 0)
@@ -246,6 +326,8 @@
         received = rows_q[...].reshape(n_slots, 128)
         gram = dot(received, received, 0, 0)
         sums[my_l] = gram[n_marks:, :] * (OWNED * n_owners / (n_points * n_owners))
+        for l, _ in l_peers:
+            pl.when(l > my_l)(functools.partial(pl.semaphore_wait, in_l.at[l], 1))
         start(s)
         totals = dot(jnp.ones((8, n_slots), BF16), received)
         count_ref[...] = pltpu.roll(totals, 128 - n_marks, 1)[:1, :OWNED].astype(I32)
@@ -259,27 +341,32 @@
             low = (whole - high.astype(F32)).astype(BF16)
             factors.append(jnp.concatenate([high, low], axis=0))
         for k in range(CHUNKS):
-            arrive(p3[k][1])
+            arrive(c3[k][1])
         for column in range(4):
-            both = dot(factors[0], panel[column])
+            both = dot(factors[0], panel[column % 2, column // 2])
             for l in range(1, nl):
-                both = both + dot(factors[l], panel[l * 4 + column])
+                both = both + dot(factors[l], panel[column % 2, l * 2 + column // 2])
             out_ref[:, column * 128 : (column + 1) * 128] = both[:OWNED] + both[OWNED:]
 
-    scatter(0)
-    rows_along_z()
-    for k in range(1, CHUNKS):
+    assign_slots()
+    kernel_rows()
+    fill_slots()
+    everyone_in()
+    for k in range(CHUNKS):
+        to_sibling(k)
+    rows_down()
+    for k in range(CHUNKS):
         scatter(k)
-    along_z(0)
+    rows_up()
+    for k in range(CHUNKS):
+        along_z(k)
     rows_in_plane()
-    for k in range(1, CHUNKS):
-        along_z(k)
-    gather(0)
+    for k in range(CHUNKS):
+        gather(k)
     sum_rows()
-    for k in range(1, CHUNKS):
-        gather(k)
+    for k in range(CHUNKS):
+        share(k)
     finish()
-
     for copy in sent:
         copy.wait_send()
 
@@ -305,6 +392,7 @@
         n_points, depth = points.shape
         n_marks = landmarks.shape[0]
         columns = panels.shape[2]
+        step = n_marks // CHUNKS
         hbm = pl.BlockSpec(memory_space=pl.ANY)
         vmem = pl.BlockSpec(memory_space=pltpu.VMEM)
         dma = pltpu.SemaphoreType.DMA
@@ -321,31 +409,39 @@
                 pltpu.VMEM((n_points, depth), BF16),
                 pltpu.VMEM((128, depth), BF16),
                 pltpu.VMEM((1, n_points), I32),
-                pltpu.VMEM((nl * n_marks, columns), BF16),
+                pltpu.VMEM((nl, n_marks, columns), BF16),
+                [pltpu.VMEM((2, 2, nx, step, 128), BF16)] * CHUNKS,
+                [pltpu.VMEM((2, nx, step, 128), BF16)] * CHUNKS,
                 pltpu.VMEM((nz, nq * CAP, 128), BF16),
                 pltpu.VMEM((nz, nq * CAP, 128), BF16),
                 pltpu.VMEM((nq, nz * CAP, 128), BF16),
                 pltpu.VMEM((nq, nz * CAP, 128), BF16),
-                [pltpu.VMEM((nq, n_marks // CHUNKS, 128), BF16)] * CHUNKS,
-                [pltpu.VMEM((nz, n_marks // CHUNKS, 128), BF16)] * CHUNKS,
-                pltpu.VMEM((nq, n_marks, 128), BF16),
+                [pltpu.VMEM((nx * 2, step, 128), BF16)] * CHUNKS,
+                [pltpu.VMEM((nz, step, 128), BF16)] * CHUNKS,
+                pltpu.VMEM((2, nx * 2, n_marks, 128), BF16),
                 pltpu.VMEM((nl, OWNED, 128), F32),
-                dma((6 + CHUNKS,)),
+                dma((6 + 2 * CHUNKS,)),
                 dma((nz,)),
                 dma((nz,)),
                 dma((nq,)),
                 dma((nq,)),
-                dma((CHUNKS, nq)),
-                dma((CHUNKS, nq)),
+                dma((CHUNKS, 2)),
+                dma((CHUNKS, 2)),
+                dma((CHUNKS, nx * 2)),
+                dma((CHUNKS, nx * 2)),
                 dma((CHUNKS, nz)),
                 dma((CHUNKS, nz)),
-                dma((CHUNKS, nq)),
-                dma((CHUNKS, nq)),
+                dma((CHUNKS, nx * 2)),
+                dma((CHUNKS, nx * 2)),
+                dma((CHUNKS,)),
+                dma((CHUNKS,)),
                 dma((nl,)),
                 dma((nl,)),
+                pltpu.SemaphoreType.REGULAR((nz,)),
+                pltpu.SemaphoreType.REGULAR((nl,)),
             ],
             compiler_params=pltpu.CompilerParams(collective_id=0, has_side_effects=True),
-        )(panel_index.reshape(1, 1), points, landmarks, panels, assignment.reshape(1, n_points))
+        )(panel_index.reshape(1, 1), points, landmarks, panels.reshape(nl, n_marks, columns), assignment.reshape(1, n_points))
         out, counts = pl.pallas_call(
             write_out,
             out_shape=(

time: 38.6 us -> 35.8 us (0.927)
  Pallas kernels: 37.1 us -> 34.1 us
    pallas_call x1, Pallas kernels: 36.5 us -> 33.4 us  [body(): pl.pallas_call(functools.partial(kernel, nx, nz, nl), out_shape=(pltpu.VM...]
where the time goes in v3:
time: 35.8 us; the launch traced here: 35.4 us
  Pallas kernels  34.1 us (95%)
  between operations  1.28 us (4%)
    pallas_call x1, Pallas kernels, body(): pl.pallas_call(functools.partial(kernel, nx, nz, nl), out_shape=(pltpu.VM...  33.4 us

profile of v3, /device:TPU:1, one launch (start us, length us, event | category | flops | bytes accessed | tf_op | source)
XLA Modules:
  0.0 35.4 jit_solution(5758022676711227914)
XLA Ops:
  1.3 33.4 %shard_map.68 = (f32[32,512]{1,0:T(8,128)S(1)}, s32[1,32]{1,0:T(1,128)S(1)}) custom-call(s32[1,1]{1,0:T(1,128)} %bitcast.4.index_hbm, bf16[256,768]{1,0:T(8,128)(2,1)} %points_hbm.1, bf16[96,768]{1,0:T(8,128)(2,1)} %marks_hbm.1, bf16[4,96,512]{2,1,0:T(8,128)(2,1)} %bitcast.5, s32[1,256]{1,0:T(1,128)} %bitcast.6), custom_call_target="tpu_custom_call" | custom-call | tf_op jit(solution)/shard_map/pallas_call | solution.py:399
  34.7 0.7 %shard_map.69 = (f32[32,512]{1,0:T(8,128)}, s32[1,32]{1,0:T(1,128)}) custom-call(f32[32,512]{1,0:T(8,128)S(1)} %get-tuple-element.6.total, s32[1,32]{1,0:T(1,128)S(1)} %get-tuple-element.7.count), custom_call_target="tpu_custom_call" | custom-call | tf_op jit(solution)/shard_map/pallas_call | solution.py:445

commit v4 on v3

--- a/solution.py
+++ b/solution.py
@@ -134,13 +134,15 @@
     def signal(semaphore, device):
         pl.semaphore_signal(semaphore, inc=1, device_id=device, device_id_type=MESH)
 
+    for load in loads[:3]:
+        load.start()
+    for _, device in plane_peers[::-1]:
+        signal(barrier, device)
     for z, device in z_peers:
         pl.when(z > my_z)(functools.partial(signal, barrier, device))
-    for _, device in plane_peers:
-        signal(barrier, device)
     for l, device in l_peers:
         pl.when(l > my_l)(functools.partial(signal, barrier, device))
-    for load in loads:
+    for load in loads[3:]:
         load.start()
 
     def remote(src, dst, send, recv, device):
@@ -308,14 +310,17 @@
 
         sent.extend(rz)
 
-    def rows_in_plane():
+    def order_rows():
         target = iota((n_slots, n_slots), 0)
         at_q, at_z, at_r = target // (nz * CAP), target // CAP % nz, target % CAP
         regroup = iota((n_slots, n_slots), 1) == (at_z * nq + at_q) * CAP + at_r
         regroup = regroup.astype(F32).astype(BF16)
+        made["regroup"] = regroup
+
+    def rows_in_plane():
         own_z.wait()
         arrive(rz_back)
-        grouped = dot(regroup, rows_z[...].reshape(n_slots, 128)).astype(BF16)
+        grouped = dot(made["regroup"], rows_z[...].reshape(n_slots, 128)).astype(BF16)
         regrouped[...] = grouped.reshape(nq, nz * CAP, 128)
         start(rq)
         own_q.start()
@@ -350,20 +355,22 @@
 
     assign_slots()
     kernel_rows()
-    fill_slots()
     everyone_in()
     for k in range(CHUNKS):
         to_sibling(k)
+    fill_slots()
     rows_down()
     for k in range(CHUNKS):
         scatter(k)
     rows_up()
+    order_rows()
     for k in range(CHUNKS):
         along_z(k)
     rows_in_plane()
-    for k in range(CHUNKS):
-        gather(k)
+    gather(0)
+    gather(1)
     sum_rows()
+    gather(2)
     for k in range(CHUNKS):
         share(k)
     finish()

time: 35.8 us -> 35.1 us (0.980)
  Pallas kernels: 34.1 us -> 33.7 us
    pallas_call x1, Pallas kernels: 33.4 us -> 33 us  [body(): pl.pallas_call(functools.partial(kernel, nx, nz, nl), out_shape=(pltpu.VM...]
where the time goes in v4:
time: 35.1 us; the launch traced here: 35 us
  Pallas kernels  33.7 us (96%)
  between operations  1.28 us (4%)
    pallas_call x1, Pallas kernels, body(): pl.pallas_call(functools.partial(kernel, nx, nz, nl), out_shape=(pltpu.VM...  33 us

profile of v4, /device:TPU:1, one launch (start us, length us, event | category | flops | bytes accessed | tf_op | source)
XLA Modules:
  0.0 35.0 jit_solution(2309054586869002590)
XLA Ops:
  1.3 33.0 %shard_map.68 = (f32[32,512]{1,0:T(8,128)S(1)}, s32[1,32]{1,0:T(1,128)S(1)}) custom-call(s32[1,1]{1,0:T(1,128)} %bitcast.4.index_hbm, bf16[256,768]{1,0:T(8,128)(2,1)} %points_hbm.1, bf16[96,768]{1,0:T(8,128)(2,1)} %marks_hbm.1, bf16[4,96,512]{2,1,0:T(8,128)(2,1)} %bitcast.5, s32[1,256]{1,0:T(1,128)} %bitcast.6), custom_call_target="tpu_custom_call" | custom-call | tf_op jit(solution)/shard_map/pallas_call | solution.py:406
  34.3 0.7 %shard_map.69 = (f32[32,512]{1,0:T(8,128)}, s32[1,32]{1,0:T(1,128)}) custom-call(f32[32,512]{1,0:T(8,128)S(1)} %get-tuple-element.6.total, s32[1,32]{1,0:T(1,128)S(1)} %get-tuple-element.7.count), custom_call_target="tpu_custom_call" | custom-call | tf_op jit(solution)/shard_map/pallas_call | solution.py:452

commit v5 on v4

--- a/solution.py
+++ b/solution.py
@@ -84,9 +84,10 @@
     n_points = points_hbm.shape[0]
 
     plane_peers = []
-    for dx in range(nx):
-        for dy in range(2):
-            for dc in range(2):
+    far_x = sorted(range(nx), key=lambda d: -min(d, nx - d))
+    for dx in far_x:
+        for dy in (1, 0):
+            for dc in (1, 0):
                 if dx or dy or dc:
                     x = (my_x + dx) % nx
                     yc = (my_y + dy) % 2 * 2 + (my_c + dc) % 2
@@ -95,8 +96,8 @@
     sibling = (me + other_c - my_c, my_l)
     my_xy = my_x * 2 + my_y
     xy_peers = []
-    for dx in range(nx):
-        for dy in range(2):
+    for dx in far_x:
+        for dy in (1, 0):
             if dx or dy:
                 x, y = (my_x + dx) % nx, (my_y + dy) % 2
                 xy_peers.append((x, y, ((x * nz + my_z) * 4 + y * 2 + my_c, my_l)))
@@ -105,7 +106,7 @@
         z = (my_z + dz) % nz
         z_peers.append((z, ((my_x * nz + z) * 4 + my_yc, my_l)))
     l_peers = []
-    for dl in range(1, nl):
+    for dl in sorted(range(1, nl), key=lambda d: -min(d, nl - d)):
         l = (my_l + dl) % nl
         l_peers.append((l, (me, l)))
 
@@ -136,7 +137,7 @@
 
     for load in loads[:3]:
         load.start()
-    for _, device in plane_peers[::-1]:
+    for _, device in plane_peers:
         signal(barrier, device)
     for z, device in z_peers:
         pl.when(z > my_z)(functools.partial(signal, barrier, device))

time: 35.1 us -> 34.7 us (0.989)
  Pallas kernels: 33.7 us -> 33.2 us
    pallas_call x1, Pallas kernels: 33 us -> 32.6 us  [body(): pl.pallas_call(functools.partial(kernel, nx, nz, nl), out_shape=(pltpu.VM...]
where the time goes in v5:
time: 34.7 us; the launch traced here: 34.5 us
  Pallas kernels  33.2 us (96%)
  between operations  1.28 us (4%)
    pallas_call x1, Pallas kernels, body(): pl.pallas_call(functools.partial(kernel, nx, nz, nl), out_shape=(pltpu.VM...  32.6 us

profile of v5, /device:TPU:1, one launch (start us, length us, event | category | flops | bytes accessed | tf_op | source)
XLA Modules:
  0.0 34.5 jit_solution(6306090824725881253)
XLA Ops:
  1.3 32.6 %shard_map.68 = (f32[32,512]{1,0:T(8,128)S(1)}, s32[1,32]{1,0:T(1,128)S(1)}) custom-call(s32[1,1]{1,0:T(1,128)} %bitcast.4.index_hbm, bf16[256,768]{1,0:T(8,128)(2,1)} %points_hbm.1, bf16[96,768]{1,0:T(8,128)(2,1)} %marks_hbm.1, bf16[4,96,512]{2,1,0:T(8,128)(2,1)} %bitcast.5, s32[1,256]{1,0:T(1,128)} %bitcast.6), custom_call_target="tpu_custom_call" | custom-call | tf_op jit(solution)/shard_map/pallas_call | solution.py:407
  33.9 0.7 %shard_map.69 = (f32[32,512]{1,0:T(8,128)}, s32[1,32]{1,0:T(1,128)}) custom-call(f32[32,512]{1,0:T(8,128)S(1)} %get-tuple-element.6.total, s32[1,32]{1,0:T(1,128)S(1)} %get-tuple-element.7.count), custom_call_target="tpu_custom_call" | custom-call | tf_op jit(solution)/shard_map/pallas_call | solution.py:453

commit v6 on v5

--- a/solution.py
+++ b/solution.py
@@ -346,21 +346,24 @@
             high = whole.astype(BF16)
             low = (whole - high.astype(F32)).astype(BF16)
             factors.append(jnp.concatenate([high, low], axis=0))
-        for k in range(CHUNKS):
-            arrive(c3[k][1])
-        for column in range(4):
-            both = dot(factors[0], panel[column % 2, column // 2])
-            for l in range(1, nl):
-                both = both + dot(factors[l], panel[column % 2, l * 2 + column // 2])
-            out_ref[:, column * 128 : (column + 1) * 128] = both[:OWNED] + both[OWNED:]
+        for c in (my_c, other_c):
+            for y in range(2):
+                both = dot(factors[0], panel[c, y])
+                for l in range(1, nl):
+                    both = both + dot(factors[l], panel[c, l * 2 + y])
+                column = pl.multiple_of((y * 2 + c) * 128, 128)
+                out_ref[:, pl.ds(column, 128)] = both[:OWNED] + both[OWNED:]
+            if c is my_c:
+                for k in range(CHUNKS):
+                    arrive(c3[k][1])
 
     assign_slots()
     kernel_rows()
+    fill_slots()
     everyone_in()
+    rows_down()
     for k in range(CHUNKS):
         to_sibling(k)
-    fill_slots()
-    rows_down()
     for k in range(CHUNKS):
         scatter(k)
     rows_up()

time: 34.7 us -> 34.7 us (level)
  no operation moved by 1% of the time
where the time goes in v6:
time: 34.7 us; the launch traced here: 34.5 us
  Pallas kernels  33.2 us (96%)
  between operations  1.28 us (4%)
    pallas_call x1, Pallas kernels, body(): pl.pallas_call(functools.partial(kernel, nx, nz, nl), out_shape=(pltpu.VM...  32.6 us

profile of v6, /device:TPU:1, one launch (start us, length us, event | category | flops | bytes accessed | tf_op | source)
XLA Modules:
  0.0 34.5 jit_solution(2664296976315339836)
XLA Ops:
  1.3 32.6 %shard_map.68 = (f32[32,512]{1,0:T(8,128)S(1)}, s32[1,32]{1,0:T(1,128)S(1)}) custom-call(s32[1,1]{1,0:T(1,128)} %bitcast.4.index_hbm, bf16[256,768]{1,0:T(8,128)(2,1)} %points_hbm.1, bf16[96,768]{1,0:T(8,128)(2,1)} %marks_hbm.1, bf16[4,96,512]{2,1,0:T(8,128)(2,1)} %bitcast.5, s32[1,256]{1,0:T(1,128)} %bitcast.6), custom_call_target="tpu_custom_call" | custom-call | tf_op jit(solution)/shard_map/pallas_call | solution.py:410
  33.9 0.7 %shard_map.69 = (f32[32,512]{1,0:T(8,128)}, s32[1,32]{1,0:T(1,128)}) custom-call(f32[32,512]{1,0:T(8,128)S(1)} %get-tuple-element.6.total, s32[1,32]{1,0:T(1,128)S(1)} %get-tuple-element.7.count), custom_call_target="tpu_custom_call" | custom-call | tf_op jit(solution)/shard_map/pallas_call | solution.py:456

commit v7 on v5

--- a/solution.py
+++ b/solution.py
@@ -356,11 +356,11 @@
 
     assign_slots()
     kernel_rows()
+    fill_slots()
     everyone_in()
+    rows_down()
     for k in range(CHUNKS):
         to_sibling(k)
-    fill_slots()
-    rows_down()
     for k in range(CHUNKS):
         scatter(k)
     rows_up()

time: 34.7 us -> 34.8 us (level)
  no operation moved by 1% of the time
where the time goes in v7:
time: 34.8 us; the launch traced here: 34.6 us
  Pallas kernels  33.3 us (96%)
  between operations  1.28 us (4%)
    pallas_call x1, Pallas kernels, body(): pl.pallas_call(functools.partial(kernel, nx, nz, nl), out_shape=(pltpu.VM...  32.7 us

profile of v7, /device:TPU:1, one launch (start us, length us, event | category | flops | bytes accessed | tf_op | source)
XLA Modules:
  0.0 34.6 jit_solution(6394495543849929773)
XLA Ops:
  1.3 32.7 %shard_map.68 = (f32[32,512]{1,0:T(8,128)S(1)}, s32[1,32]{1,0:T(1,128)S(1)}) custom-call(s32[1,1]{1,0:T(1,128)} %bitcast.4.index_hbm, bf16[256,768]{1,0:T(8,128)(2,1)} %points_hbm.1, bf16[96,768]{1,0:T(8,128)(2,1)} %marks_hbm.1, bf16[4,96,512]{2,1,0:T(8,128)(2,1)} %bitcast.5, s32[1,256]{1,0:T(1,128)} %bitcast.6), custom_call_target="tpu_custom_call" | custom-call | tf_op jit(solution)/shard_map/pallas_call | solution.py:407
  34.0 0.7 %shard_map.69 = (f32[32,512]{1,0:T(8,128)}, s32[1,32]{1,0:T(1,128)}) custom-call(f32[32,512]{1,0:T(8,128)S(1)} %get-tuple-element.6.total, s32[1,32]{1,0:T(1,128)S(1)} %get-tuple-element.7.count), custom_call_target="tpu_custom_call" | custom-call | tf_op jit(solution)/shard_map/pallas_call | solution.py:453
